TPU v7x, 32 devices: a whole 2x2x4 slice. The times are simulated.
32 devices in a mesh: grp: 2 (over y), frm: 4 (over z), row: 2 (over x), sub: 2 (over core).
Axes of the slice: x: 2, y: 2, z: 4, core: 2. Of those that a mesh axis runs over, the one named last changes fastest.
Arguments:
- signal: bfloat16 [64, 65536], P('row', ('grp', 'frm', 'sub')), parts along dimension 1, may hold values from -6 to 6
- w_start: float32 [2560, 32], P('row'), may hold values from 0.02 to 0.4
- h_start: float32 [32, 65536], P(None, ('grp', 'frm', 'sub')), parts along dimension 1, may hold values from 0.02 to 0.4
Outputs:
- synergies: float32 [5120, 32], P(('grp', 'row')), parts along dimension 0
- activations: float32 [32, 65536], P(None, ('grp', 'frm', 'sub')), parts along dimension 1
There are 2 independent parts, one for each index of `grp`. A program takes and returns all parts, laid end to end along the dimension named above; an argument that names none is the same for every part. Nothing has to cross between parts.
All inputs are finite; a program needn't handle non-finite values.
Results may differ from a plain program's by a relative error of at most 0.0019.
Values may be sent and summed in bfloat16 or wider, within the bound.
A program may use at most 128 MiB of HBM per device.

v0:
```python
import functools
import math

import jax
import jax.numpy as jnp
import numpy as np
from jax import lax
from jax.experimental import pallas as pl
from jax.experimental.pallas import tpu as pltpu
from jax.sharding import PartitionSpec as P

NF = 40
TAPS = 128
ITERS = 2
CHUNKS = 4
UNROLL = 4
HIGH = lax.Precision.HIGHEST
MESH = pl.DeviceIdType.MESH
F32, BF16 = jnp.float32, jnp.bfloat16
LANES = (((1,), (1,)), ((), ()))


def circulants():
    freq = 2.0 * 12.0 ** (np.arange(NF) / (NF - 1))
    sigma = 7.0 / (2.0 * math.pi * freq)
    times = (np.arange(TAPS) - TAPS // 2) / 50.0
    env = np.exp(-(times[None, :] ** 2) / (2.0 * sigma[:, None] ** 2))
    env = env / np.sqrt(np.sum(env * env, axis=1, keepdims=True))
    phase = 2.0 * math.pi * freq[:, None] * times[None, :]
    taps = np.stack([env * np.cos(phase), env * np.sin(phase)], axis=1).astype(np.float32)
    at = np.arange(TAPS)
    table = taps[:, :, (at[:, None] - at[None, :]) % TAPS]
    return table.transpose(0, 2, 1, 3).reshape(NF, TAPS, 2 * TAPS).astype(BF16)


def kernel(
    sizes,
    sig_ref, w_ref, h_ref, circ_ref,
    w_out, h_out,
    circ, table, halo, lhs, spec, sums, grams, acc, subs, parts, wt,
    circ_sem, halo_send, halo_recv, sum_send, sum_recv, gram_send, gram_recv,
    sub_send, sub_recv, part_send, part_recv, w_send, w_recv,
):
    nfrm, nrow, nsub = sizes
    frm, row, sub = lax.axis_index("frm"), lax.axis_index("row"), lax.axis_index("sub")
    channels, frames = sig_ref.shape
    rank, rows = w_ref.shape
    half = rank // nsub
    blocks = frames // TAPS
    per = blocks // CHUNKS
    wide = frames // CHUNKS
    place = frm * nsub + sub
    has_left, has_right = place > 0, place < nfrm * nsub - 1
    sent = []

    load = pltpu.make_async_copy(circ_ref, circ, circ_sem)
    load.start()

    def peer(name, step):
        size = {"frm": nfrm, "row": nrow, "sub": nsub}[name]
        return lax.rem(lax.axis_index(name) + step, size)

    def neighbour(side):
        at = place + side
        return {"frm": at // nsub, "sub": lax.rem(at, nsub)}

    grams[...] = jnp.zeros_like(grams)
    acc[...] = jnp.zeros_like(acc)
    wt[0] = w_ref[...]

    barrier = pltpu.get_barrier_semaphore()
    for name, size in (("frm", nfrm), ("row", nrow), ("sub", nsub)):
        for step in range(1, size):
            pl.semaphore_signal(barrier, inc=1, device_id={name: peer(name, step)}, device_id_type=MESH)

    @pl.when(has_left)
    def _():
        pl.semaphore_signal(barrier, inc=1, device_id=neighbour(-1), device_id_type=MESH)

    @pl.when(has_right)
    def _():
        pl.semaphore_signal(barrier, inc=1, device_id=neighbour(1), device_id_type=MESH)

    sides = has_left.astype(jnp.int32) + has_right.astype(jnp.int32)
    pl.semaphore_wait(barrier, nfrm + nrow + nsub - 3 + sides)

    def push(src, dst, send, recv, to):
        copy = pltpu.make_async_remote_copy(
            src_ref=src, dst_ref=dst, send_sem=send, recv_sem=recv, device_id=to, device_id_type=MESH
        )
        copy.start()
        sent.append(copy)
        return copy

    def edge(side):
        return pltpu.make_async_remote_copy(
            src_ref=sig_ref.at[:, pl.ds(frames - TAPS, TAPS)] if side > 0 else sig_ref.at[:, pl.ds(0, TAPS)],
            dst_ref=halo.at[0 if side > 0 else 1],
            send_sem=halo_send.at[0 if side > 0 else 1],
            recv_sem=halo_recv.at[0 if side > 0 else 1],
            device_id=neighbour(side),
            device_id_type=MESH,
        )

    @pl.when(has_right)
    def _():
        edge(1).start()

    @pl.when(has_left)
    def _():
        edge(-1).start()

    @pl.when(jnp.logical_not(has_left))
    def _():
        halo[0] = jnp.zeros((channels, TAPS), BF16)

    @pl.when(jnp.logical_not(has_right))
    def _():
        halo[1] = jnp.zeros((channels, TAPS), BF16)

    def share_gram(it):
        now = wt[it]
        grams[it, row, :, 0:rank] = lax.dot_general(now, now, LANES, precision=HIGH, preferred_element_type=F32)
        return [
            push(grams.at[it, row], grams.at[it, row], gram_send.at[it, s - 1], gram_recv.at[it, s - 1], {"row": peer("row", s)})
            for s in range(1, nrow)
        ]

    gram_copies = share_gram(0)

    load.wait()
    source = lax.broadcasted_iota(jnp.int32, (TAPS, 2 * TAPS), 0)
    target = lax.rem(lax.broadcasted_iota(jnp.int32, (TAPS, 2 * TAPS), 1), TAPS)
    lead = jnp.where(source >= target, 1.0, 0.0).astype(BF16)
    trail = jnp.where(source >= target, 0.0, 1.0).astype(BF16)

    def fill(f, carry):
        table[f, 0:TAPS, :] = circ[f] * lead
        table[f, TAPS : 2 * TAPS, :] = circ[f] * trail
        return carry

    lax.fori_loop(0, NF, fill, 0)

    @pl.when(has_left)
    def _():
        edge(1).wait_recv()

    @pl.when(has_right)
    def _():
        edge(-1).wait_recv()

    low_half = lax.broadcasted_iota(jnp.int32, (channels, TAPS), 1) < TAPS // 2
    before = pltpu.roll(halo[0].astype(F32), TAPS // 2, 1)
    for i in range(blocks + 1):
        after = sig_ref[:, i * TAPS : (i + 1) * TAPS] if i < blocks else halo[1]
        after = pltpu.roll(after.astype(F32), TAPS // 2, 1)
        piece = jnp.where(low_half, before, after).astype(BF16)
        if i < blocks:
            lhs[i * channels : (i + 1) * channels, 0:TAPS] = piece
        if i > 0:
            lhs[(i - 1) * channels : i * channels, TAPS : 2 * TAPS] = piece
        before = after

    def wavelets(q):
        first = q * per

        def group(g, carry):
            for u in range(UNROLL):
                f = g * UNROLL + u
                out = jnp.dot(
                    lhs[first * channels : (first + per) * channels, :], table[f], preferred_element_type=F32
                )
                power = (out[:, :TAPS] * out[:, :TAPS] + out[:, TAPS:] * out[:, TAPS:]).astype(BF16)
                at = pl.multiple_of(f * channels, channels)
                for b in range(per):
                    spec[pl.ds(at, channels), (first + b) * TAPS : (first + b + 1) * TAPS] = power[
                        b * channels : (b + 1) * channels
                    ]
            return carry

        lax.fori_loop(0, NF // UNROLL, group, 0)

    def project(it, q, w_low):
        sums[it, row, q] = jnp.dot(w_low, spec[:, q * wide : (q + 1) * wide], preferred_element_type=F32)
        return [
            push(
                sums.at[it, row, q], sums.at[it, row, q],
                sum_send.at[it, q, s - 1], sum_recv.at[it, q, s - 1], {"row": peer("row", s)},
            )
            for s in range(1, nrow)
        ]

    def update_h(it, q, copies, gram):
        for copy in copies:
            copy.wait_recv()
        total = sums[it, 0, q]
        for s in range(1, nrow):
            total = total + sums[it, s, q]
        cols = slice(q * wide, (q + 1) * wide)
        old = h_ref[:, cols] if it == 0 else h_out[:, cols]
        new = old * total / jnp.dot(gram, old, precision=HIGH, preferred_element_type=F32)
        h_out[:, cols] = new
        acc[it, :, 0:rows] += lax.dot_general(new.astype(BF16), spec[:, cols], LANES, preferred_element_type=F32)
        acc[it, :, rows : rows + rank] += lax.dot_general(new, new, LANES, precision=HIGH, preferred_element_type=F32)

    def whole_gram(it, copies):
        for copy in copies:
            copy.wait_recv()
        total = grams[it, 0, :, 0:rank]
        for s in range(1, nrow):
            total = total + grams[it, s, :, 0:rank]
        return total

    def update_w(it):
        copies = []
        for s in range(1, nsub):
            theirs = pl.multiple_of(peer("sub", s) * half, half)
            copies.append(
                push(acc.at[it, pl.ds(theirs, half)], subs.at[it, s - 1], sub_send.at[it, s - 1], sub_recv.at[it, s - 1], {"sub": peer("sub", s)})
            )
        mine = pl.ds(pl.multiple_of(sub * half, half), half)
        for copy in copies:
            copy.wait_recv()
        chip = acc[it, mine, :]
        for s in range(1, nsub):
            chip = chip + subs[it, s - 1]
        parts[it, frm, :, 0:rows] = chip[:, :rows].astype(BF16)
        fine = chip[:, rows:]
        coarse = fine.astype(BF16)
        parts[it, frm, :, rows : rows + 128] = coarse
        parts[it, frm, :, rows + 128 : rows + 256] = (fine - coarse.astype(F32)).astype(BF16)
        copies = [
            push(parts.at[it, frm], parts.at[it, frm], part_send.at[it, s - 1], part_recv.at[it, s - 1], {"frm": peer("frm", s)})
            for s in range(1, nfrm)
        ]
        for copy in copies:
            copy.wait_recv()
        total = parts[it, 0].astype(F32)
        for s in range(1, nfrm):
            total = total + parts[it, s].astype(F32)
        gram = total[:, rows : rows + rank] + total[:, rows + 128 : rows + 128 + rank]
        den = jnp.dot(gram, wt[it], precision=HIGH, preferred_element_type=F32)
        wt[it + 1, mine, :] = wt[it, mine, :] * total[:, :rows] / den
        copies = [
            push(wt.at[it + 1, mine], wt.at[it + 1, mine], w_send.at[it, s - 1], w_recv.at[it, s - 1], {"sub": peer("sub", s)})
            for s in range(1, nsub)
        ]
        for copy in copies:
            copy.wait_recv()

    for it in range(ITERS):
        w_low = wt[it].astype(BF16)
        if it:
            gram_copies = share_gram(it)
        waiting = []
        gram = None
        for q in range(CHUNKS):
            if it == 0:
                wavelets(q)
            waiting.append(project(it, q, w_low))
            if it == 0 and q >= 2:
                if gram is None:
                    gram = whole_gram(it, gram_copies)
                update_h(it, q - 2, waiting[q - 2], gram)
        if gram is None:
            gram = whole_gram(it, gram_copies)
        for q in range(CHUNKS - 2 if it == 0 else 0, CHUNKS):
            update_h(it, q, waiting[q], gram)
        update_w(it)
    w_out[...] = wt[ITERS]

    for copy in sent:
        copy.wait_send()

    @pl.when(has_right)
    def _():
        edge(1).wait_send()

    @pl.when(has_left)
    def _():
        edge(-1).wait_send()


def solution(mesh):
    sizes = nfrm, nrow, nsub = tuple(mesh.shape[name] for name in ("frm", "row", "sub"))
    circ = circulants()

    def shards(signal, w_start, h_start):
        channels, frames = signal.shape
        rows, rank = w_start.shape
        half = rank // nsub
        wide = frames // CHUNKS
        w = w_start.reshape(channels, NF, rank).transpose(2, 1, 0).reshape(rank, rows)
        dma = pltpu.SemaphoreType.DMA
        vmem = pl.BlockSpec(memory_space=pltpu.VMEM)
        w, h = pl.pallas_call(
            functools.partial(kernel, sizes),
            out_shape=(
                jax.ShapeDtypeStruct((rank, rows), F32),
                jax.ShapeDtypeStruct((rank, frames), F32),
            ),
            in_specs=[vmem, vmem, vmem, pl.BlockSpec(memory_space=pl.ANY)],
            out_specs=(vmem, vmem),
            scratch_shapes=[
                pltpu.VMEM((NF, TAPS, 2 * TAPS), BF16),
                pltpu.VMEM((NF, 2 * TAPS, 2 * TAPS), BF16),
                pltpu.VMEM((2, channels, TAPS), BF16),
                pltpu.VMEM((frames // TAPS * channels, 2 * TAPS), BF16),
                pltpu.VMEM((rows, frames), BF16),
                pltpu.VMEM((ITERS, nrow, CHUNKS, rank, wide), F32),
                pltpu.VMEM((ITERS, nrow, rank, 128), F32),
                pltpu.VMEM((ITERS, rank, rows + 128), F32),
                pltpu.VMEM((ITERS, nsub - 1, half, rows + 128), F32),
                pltpu.VMEM((ITERS, nfrm, half, rows + 256), BF16),
                pltpu.VMEM((ITERS + 1, rank, rows), F32),
                dma,
                dma((2,)), dma((2,)),
                dma((ITERS, CHUNKS, nrow - 1)), dma((ITERS, CHUNKS, nrow - 1)),
                dma((ITERS, nrow - 1)), dma((ITERS, nrow - 1)),
                dma((ITERS, nsub - 1)), dma((ITERS, nsub - 1)),
                dma((ITERS, nfrm - 1)), dma((ITERS, nfrm - 1)),
                dma((ITERS, nsub - 1)), dma((ITERS, nsub - 1)),
            ],
            compiler_params=pltpu.CompilerParams(
                collective_id=0, has_side_effects=True, vmem_limit_bytes=56 << 20
            ),
        )(signal, w, h_start, jnp.asarray(circ))
        return w.reshape(rank, NF, channels).transpose(2, 1, 0).reshape(rows, rank), h

    return jax.shard_map(
        shards,
        mesh=mesh,
        in_specs=(P("row", ("grp", "frm", "sub")), P("row", None), P(None, ("grp", "frm", "sub"))),
        out_specs=(P(("grp", "row"), None), P(None, ("grp", "frm", "sub"))),
        check_vma=False,
    )
```

profile of v0, /device:TPU:0, one launch (start us, length us, event | category | flops | bytes accessed | tf_op | source)
XLA Modules:
  0.0 67.8 jit_solution(591723734491461252)
XLA Ops:
  0.6 1.3 %reshape.16 = f32[32,40,32]{1,0,2:T(8,128)S(1)} reshape(f32[1280,32]{0,1:T(8,128)} %param.5) | data formatting | bytes 327680 | tf_op jit(solution)/shard_map/reshape | solution.py:293
  1.9 0.3 copy.9
  2.2 0.9 %reshape.17.w_ref = f32[32,1280]{1,0:T(8,128)} reshape(f32[32,40,32]{2,1,0:T(8,128)S(1)} %bitcast.6) | data formatting | bytes 327680 | tf_op jit(solution)/shard_map/reshape | solution.py:293
  3.1 61.5 %shard_map.59 = (f32[32,1280]{1,0:T(8,128)}, f32[32,4096]{1,0:T(8,128)}) custom-call(bf16[32,4096]{1,0:T(8,128)(2,1)} %sig_ref.1, f32[32,1280]{1,0:T(8,128)} %reshape.17.w_ref, f32[32,4096]{1,0:T(8,128)} %h_ref.1, bf16[40,128,256]{2,1,0:T(8,128)(2,1)} %constant.2.clone.circ_ref), custom_call_target="tpu_custom_call" | custom-call | tf_op jit(solution)/shard_map/pallas_call | solution.py:296
  64.6 0.0 copy-start
  64.6 1.2 %reshape.18 = f32[32,40,32]{2,1,0:T(8,128)S(1)} reshape(f32[32,1280]{1,0:T(8,128)} %get-tuple-element.4) | data formatting | bytes 327680 | tf_op jit(solution)/shard_map/reshape | solution.py:328
  65.8 0.2 copy.10
  66.0 1.0 %reshape.19 = f32[1280,32]{0,1:T(8,128)} reshape(f32[32,40,32]{1,0,2:T(8,128)S(1)} %copy.10) | data formatting | bytes 327680 | tf_op jit(solution)/shard_map/reshape | solution.py:328
  67.0 0.0 copy-done
  67.0 0.8 %copy.12 = f32[32,4096]{1,0:T(8,128)} copy(f32[32,4096]{1,0:T(8,128)S(1)} %copy-done) | data formatting | bytes 1048576
Async XLA Ops:
  64.6 2.4 %copy-start = (f32[32,4096]{1,0:T(8,128)S(1)}, f32[32,4096]{1,0:T(8,128)}, u32[]{:S(2)}) copy-start(f32[32,4096]{1,0:T(8,128)} %get-tuple-element.9) | copy-start | bytes 1572868
where the time goes:
time: 67.9 us; the launch traced here: 67.8 us
  Pallas kernels  61.5 us (91%)
  local copies, waits for them, and re-layouts  5.59 us (8%)
    pallas_call x1, Pallas kernels, shards(): pl.pallas_call(functools.partial(kernel, sizes), out_shape=(jax.ShapeDtyp...  61.5 us
    reshape x3, local copies, waits for them, and re-layouts, shards(): w_start.reshape(channels, NF, rank).transpose(2, 1, 0).reshape(rank, rows)  2.43 us
    reshape x2, local copies, waits for them, and re-layouts, shards(): w.reshape(rank, NF, channels).transpose(2, 1, 0).reshape(rows, rank)  2.15 us

commit v1 on v0

--- a/solution.py
+++ b/solution.py
@@ -37,7 +37,7 @@
     sizes,
     sig_ref, w_ref, h_ref, circ_ref,
     w_out, h_out,
-    circ, table, halo, lhs, spec, sums, grams, acc, subs, parts, wt,
+    circ, table, halo, lhs, spec, ratios, sums, grams, acc, subs, parts, wt,
     circ_sem, halo_send, halo_recv, sum_send, sum_recv, gram_send, gram_recv,
     sub_send, sub_recv, part_send, part_recv, w_send, w_recv,
 ):
@@ -81,9 +81,6 @@
     def _():
         pl.semaphore_signal(barrier, inc=1, device_id=neighbour(1), device_id_type=MESH)
 
-    sides = has_left.astype(jnp.int32) + has_right.astype(jnp.int32)
-    pl.semaphore_wait(barrier, nfrm + nrow + nsub - 3 + sides)
-
     def push(src, dst, send, recv, to):
         copy = pltpu.make_async_remote_copy(
             src_ref=src, dst_ref=dst, send_sem=send, recv_sem=recv, device_id=to, device_id_type=MESH
@@ -102,22 +99,6 @@
             device_id_type=MESH,
         )
 
-    @pl.when(has_right)
-    def _():
-        edge(1).start()
-
-    @pl.when(has_left)
-    def _():
-        edge(-1).start()
-
-    @pl.when(jnp.logical_not(has_left))
-    def _():
-        halo[0] = jnp.zeros((channels, TAPS), BF16)
-
-    @pl.when(jnp.logical_not(has_right))
-    def _():
-        halo[1] = jnp.zeros((channels, TAPS), BF16)
-
     def share_gram(it):
         now = wt[it]
         grams[it, row, :, 0:rank] = lax.dot_general(now, now, LANES, precision=HIGH, preferred_element_type=F32)
@@ -126,40 +107,68 @@
             for s in range(1, nrow)
         ]
 
-    gram_copies = share_gram(0)
-
-    load.wait()
-    source = lax.broadcasted_iota(jnp.int32, (TAPS, 2 * TAPS), 0)
-    target = lax.rem(lax.broadcasted_iota(jnp.int32, (TAPS, 2 * TAPS), 1), TAPS)
-    lead = jnp.where(source >= target, 1.0, 0.0).astype(BF16)
-    trail = jnp.where(source >= target, 0.0, 1.0).astype(BF16)
-
-    def fill(f, carry):
-        table[f, 0:TAPS, :] = circ[f] * lead
-        table[f, TAPS : 2 * TAPS, :] = circ[f] * trail
-        return carry
-
-    lax.fori_loop(0, NF, fill, 0)
-
-    @pl.when(has_left)
-    def _():
-        edge(1).wait_recv()
-
-    @pl.when(has_right)
-    def _():
-        edge(-1).wait_recv()
+    @pl.when(jnp.logical_not(has_left))
+    def _():
+        halo[0] = jnp.zeros((channels, TAPS), BF16)
+
+    @pl.when(jnp.logical_not(has_right))
+    def _():
+        halo[1] = jnp.zeros((channels, TAPS), BF16)
+
+    def greet():
+        sides = has_left.astype(jnp.int32) + has_right.astype(jnp.int32)
+        pl.semaphore_wait(barrier, nfrm + nrow + nsub - 3 + sides)
+
+        @pl.when(has_right)
+        def _():
+            edge(1).start()
+
+        @pl.when(has_left)
+        def _():
+            edge(-1).start()
 
     low_half = lax.broadcasted_iota(jnp.int32, (channels, TAPS), 1) < TAPS // 2
-    before = pltpu.roll(halo[0].astype(F32), TAPS // 2, 1)
-    for i in range(blocks + 1):
-        after = sig_ref[:, i * TAPS : (i + 1) * TAPS] if i < blocks else halo[1]
-        after = pltpu.roll(after.astype(F32), TAPS // 2, 1)
+
+    def turned(block):
+        return pltpu.roll(block.astype(F32), TAPS // 2, 1)
+
+    def window(i, before, after):
         piece = jnp.where(low_half, before, after).astype(BF16)
         if i < blocks:
             lhs[i * channels : (i + 1) * channels, 0:TAPS] = piece
         if i > 0:
             lhs[(i - 1) * channels : i * channels, TAPS : 2 * TAPS] = piece
+
+    before = turned(sig_ref[:, 0:TAPS])
+    for i in range(1, blocks):
+        after = turned(sig_ref[:, i * TAPS : (i + 1) * TAPS])
+        window(i, before, after)
         before = after
+
+    def outer_windows():
+        @pl.when(has_left)
+        def _():
+            edge(1).wait_recv()
+
+        @pl.when(has_right)
+        def _():
+            edge(-1).wait_recv()
+
+        window(0, turned(halo[0]), turned(sig_ref[:, 0:TAPS]))
+        window(blocks, turned(sig_ref[:, frames - TAPS : frames]), turned(halo[1]))
+
+    source = lax.broadcasted_iota(jnp.int32, (TAPS, 2 * TAPS), 0)
+    target = lax.rem(lax.broadcasted_iota(jnp.int32, (TAPS, 2 * TAPS), 1), TAPS)
+    lead = jnp.where(source >= target, 1.0, 0.0).astype(BF16)
+    trail = jnp.where(source >= target, 0.0, 1.0).astype(BF16)
+    load.wait()
+
+    def fill(f, carry):
+        table[f, 0:TAPS, :] = circ[f] * lead
+        table[f, TAPS : 2 * TAPS, :] = circ[f] * trail
+        return carry
+
+    lax.fori_loop(0, NF, fill, 0)
 
     def wavelets(q):
         first = q * per
@@ -181,27 +190,44 @@
         lax.fori_loop(0, NF // UNROLL, group, 0)
 
     def project(it, q, w_low):
-        sums[it, row, q] = jnp.dot(w_low, spec[:, q * wide : (q + 1) * wide], preferred_element_type=F32)
+        value = jnp.dot(w_low, spec[:, q * wide : (q + 1) * wide], preferred_element_type=F32)
+        coarse = value.astype(BF16)
+        sums[it, 0, row, q] = coarse
+        sums[it, 1, row, q] = (value - coarse.astype(F32)).astype(BF16)
+
+    def share_sums(it, part, q):
         return [
             push(
-                sums.at[it, row, q], sums.at[it, row, q],
-                sum_send.at[it, q, s - 1], sum_recv.at[it, q, s - 1], {"row": peer("row", s)},
+                sums.at[it, part, row, q], sums.at[it, part, row, q],
+                sum_send.at[it, part, q, s - 1], sum_recv.at[it, part, q, s - 1], {"row": peer("row", s)},
             )
             for s in range(1, nrow)
         ]
 
-    def update_h(it, q, copies, gram):
-        for copy in copies:
-            copy.wait_recv()
-        total = sums[it, 0, q]
-        for s in range(1, nrow):
-            total = total + sums[it, s, q]
+    def ratio(it, q, gram):
         cols = slice(q * wide, (q + 1) * wide)
         old = h_ref[:, cols] if it == 0 else h_out[:, cols]
-        new = old * total / jnp.dot(gram, old, precision=HIGH, preferred_element_type=F32)
-        h_out[:, cols] = new
+        ratios[:, cols] = old / jnp.dot(gram, old, precision=HIGH, preferred_element_type=F32)
+
+    def update_h(it, q, copies):
+        for copy in copies:
+            copy.wait_recv()
+        total = sums[it, 0, 0, q].astype(F32)
+        for s in range(1, nrow):
+            total = total + sums[it, 0, s, q].astype(F32)
+        cols = slice(q * wide, (q + 1) * wide)
+        new = ratios[:, cols] * total
         acc[it, :, 0:rows] += lax.dot_general(new.astype(BF16), spec[:, cols], LANES, preferred_element_type=F32)
         acc[it, :, rows : rows + rank] += lax.dot_general(new, new, LANES, precision=HIGH, preferred_element_type=F32)
+
+    def finish_h(it, q, copies):
+        for copy in copies:
+            copy.wait_recv()
+        total = sums[it, 0, 0, q].astype(F32) + sums[it, 1, 0, q].astype(F32)
+        for s in range(1, nrow):
+            total = total + (sums[it, 0, s, q].astype(F32) + sums[it, 1, s, q].astype(F32))
+        cols = slice(q * wide, (q + 1) * wide)
+        h_out[:, cols] = ratios[:, cols] * total
 
     def whole_gram(it, copies):
         for copy in copies:
@@ -211,7 +237,7 @@
             total = total + grams[it, s, :, 0:rank]
         return total
 
-    def update_w(it):
+    def update_w(it, meanwhile):
         copies = []
         for s in range(1, nsub):
             theirs = pl.multiple_of(peer("sub", s) * half, half)
@@ -226,19 +252,19 @@
             chip = chip + subs[it, s - 1]
         parts[it, frm, :, 0:rows] = chip[:, :rows].astype(BF16)
         fine = chip[:, rows:]
-        coarse = fine.astype(BF16)
-        parts[it, frm, :, rows : rows + 128] = coarse
-        parts[it, frm, :, rows + 128 : rows + 256] = (fine - coarse.astype(F32)).astype(BF16)
+        coarse = fine.astype(BF16).astype(F32)
+        parts[it, frm, :, rows:] = (coarse + pltpu.roll(fine - coarse, rank, 1)).astype(BF16)
         copies = [
             push(parts.at[it, frm], parts.at[it, frm], part_send.at[it, s - 1], part_recv.at[it, s - 1], {"frm": peer("frm", s)})
             for s in range(1, nfrm)
         ]
+        meanwhile()
         for copy in copies:
             copy.wait_recv()
         total = parts[it, 0].astype(F32)
         for s in range(1, nfrm):
             total = total + parts[it, s].astype(F32)
-        gram = total[:, rows : rows + rank] + total[:, rows + 128 : rows + 128 + rank]
+        gram = (total[:, rows:] + pltpu.roll(total[:, rows:], 128 - rank, 1))[:, :rank]
         den = jnp.dot(gram, wt[it], precision=HIGH, preferred_element_type=F32)
         wt[it + 1, mine, :] = wt[it, mine, :] * total[:, :rows] / den
         copies = [
@@ -248,25 +274,50 @@
         for copy in copies:
             copy.wait_recv()
 
+    order = [*range(1, CHUNKS - 1), 0, CHUNKS - 1]
     for it in range(ITERS):
         w_low = wt[it].astype(BF16)
-        if it:
+        leading, trailing = {}, {}
+        if it == 0:
+            wavelets(order[0])
+            greet()
             gram_copies = share_gram(it)
-        waiting = []
-        gram = None
-        for q in range(CHUNKS):
-            if it == 0:
-                wavelets(q)
-            waiting.append(project(it, q, w_low))
-            if it == 0 and q >= 2:
-                if gram is None:
-                    gram = whole_gram(it, gram_copies)
-                update_h(it, q - 2, waiting[q - 2], gram)
-        if gram is None:
+            gram = None
+            for k, q in enumerate(order):
+                if k:
+                    if k == len(order) - 2:
+                        outer_windows()
+                    wavelets(q)
+                project(it, q, w_low)
+                leading[q] = share_sums(it, 0, q)
+                if k:
+                    if gram is None:
+                        gram = whole_gram(it, gram_copies)
+                    trailing[order[k - 1]] = share_sums(it, 1, order[k - 1])
+                    ratio(it, order[k - 1], gram)
+                    update_h(it, order[k - 1], leading[order[k - 1]])
+            last = order[-1:]
+            ratio(it, last[0], gram)
+        else:
+            gram_copies = share_gram(it)
+            for q in order:
+                project(it, q, w_low)
+                leading[q] = share_sums(it, 0, q)
             gram = whole_gram(it, gram_copies)
-        for q in range(CHUNKS - 2 if it == 0 else 0, CHUNKS):
-            update_h(it, q, waiting[q], gram)
-        update_w(it)
+            last = order
+            for q in order:
+                ratio(it, q, gram)
+        for q in order:
+            if q not in trailing:
+                trailing[q] = share_sums(it, 1, q)
+        for q in last:
+            update_h(it, q, leading[q])
+
+        def meanwhile():
+            for q in order:
+                finish_h(it, q, trailing[q])
+
+        update_w(it, meanwhile)
     w_out[...] = wt[ITERS]
 
     for copy in sent:
@@ -307,15 +358,16 @@
                 pltpu.VMEM((2, channels, TAPS), BF16),
                 pltpu.VMEM((frames // TAPS * channels, 2 * TAPS), BF16),
                 pltpu.VMEM((rows, frames), BF16),
-                pltpu.VMEM((ITERS, nrow, CHUNKS, rank, wide), F32),
+                pltpu.VMEM((rank, frames), F32),
+                pltpu.VMEM((ITERS, 2, nrow, CHUNKS, rank, wide), BF16),
                 pltpu.VMEM((ITERS, nrow, rank, 128), F32),
                 pltpu.VMEM((ITERS, rank, rows + 128), F32),
                 pltpu.VMEM((ITERS, nsub - 1, half, rows + 128), F32),
-                pltpu.VMEM((ITERS, nfrm, half, rows + 256), BF16),
+                pltpu.VMEM((ITERS, nfrm, half, rows + 128), BF16),
                 pltpu.VMEM((ITERS + 1, rank, rows), F32),
                 dma,
                 dma((2,)), dma((2,)),
-                dma((ITERS, CHUNKS, nrow - 1)), dma((ITERS, CHUNKS, nrow - 1)),
+                dma((ITERS, 2, CHUNKS, nrow - 1)), dma((ITERS, 2, CHUNKS, nrow - 1)),
                 dma((ITERS, nrow - 1)), dma((ITERS, nrow - 1)),
                 dma((ITERS, nsub - 1)), dma((ITERS, nsub - 1)),
                 dma((ITERS, nfrm - 1)), dma((ITERS, nfrm - 1)),

time: 67.9 us -> 61.8 us (0.910)
  Pallas kernels: 61.5 us -> 55.4 us
    pallas_call x1, Pallas kernels: 61.5 us -> 55.4 us  [shards(): pl.pallas_call(functools.partial(kernel, sizes), out_shape=(jax.ShapeDtyp...]
where the time goes in v1:
time: 61.8 us; the launch traced here: 61.6 us
  Pallas kernels  55.4 us (90%)
  local copies, waits for them, and re-layouts  5.59 us (9%)
  between operations  0.67 us (1%)
    pallas_call x1, Pallas kernels, shards(): pl.pallas_call(functools.partial(kernel, sizes), out_shape=(jax.ShapeDtyp...  55.4 us
    reshape x3, local copies, waits for them, and re-layouts, shards(): w_start.reshape(channels, NF, rank).transpose(2, 1, 0).reshape(rank, rows)  2.43 us
    reshape x2, local copies, waits for them, and re-layouts, shards(): w.reshape(rank, NF, channels).transpose(2, 1, 0).reshape(rows, rank)  2.15 us

profile of v1, /device:TPU:0, one launch (start us, length us, event | category | flops | bytes accessed | tf_op | source)
XLA Modules:
  0.0 61.6 jit_solution(13045309581493938034)
XLA Ops:
  0.6 1.3 %reshape.16 = f32[32,40,32]{1,0,2:T(8,128)S(1)} reshape(f32[1280,32]{0,1:T(8,128)} %param.5) | data formatting | bytes 327680 | tf_op jit(solution)/shard_map/reshape | solution.py:344
  1.9 0.3 copy.9
  2.2 0.9 %reshape.17.w_ref = f32[32,1280]{1,0:T(8,128)} reshape(f32[32,40,32]{2,1,0:T(8,128)S(1)} %bitcast.6) | data formatting | bytes 327680 | tf_op jit(solution)/shard_map/reshape | solution.py:344
  3.1 55.4 %shard_map.59 = (f32[32,1280]{1,0:T(8,128)}, f32[32,4096]{1,0:T(8,128)}) custom-call(bf16[32,4096]{1,0:T(8,128)(2,1)} %sig_ref.1, f32[32,1280]{1,0:T(8,128)} %reshape.17.w_ref, f32[32,4096]{1,0:T(8,128)} %h_ref.1, bf16[40,128,256]{2,1,0:T(8,128)(2,1)} %constant.2.clone.circ_ref), custom_call_target="tpu_custom_call" | custom-call | tf_op jit(solution)/shard_map/pallas_call | solution.py:347
  58.4 0.0 copy-start
  58.4 1.2 %reshape.18 = f32[32,40,32]{2,1,0:T(8,128)S(1)} reshape(f32[32,1280]{1,0:T(8,128)} %get-tuple-element.4) | data formatting | bytes 327680 | tf_op jit(solution)/shard_map/reshape | solution.py:380
  59.6 0.2 copy.10
  59.9 1.0 %reshape.19 = f32[1280,32]{0,1:T(8,128)} reshape(f32[32,40,32]{1,0,2:T(8,128)S(1)} %copy.10) | data formatting | bytes 327680 | tf_op jit(solution)/shard_map/reshape | solution.py:380
  60.8 0.0 copy-done
  60.8 0.8 %copy.12 = f32[32,4096]{1,0:T(8,128)} copy(f32[32,4096]{1,0:T(8,128)S(1)} %copy-done) | data formatting | bytes 1048576
Async XLA Ops:
  58.4 2.4 %copy-start = (f32[32,4096]{1,0:T(8,128)S(1)}, f32[32,4096]{1,0:T(8,128)}, u32[]{:S(2)}) copy-start(f32[32,4096]{1,0:T(8,128)} %get-tuple-element.9) | copy-start | bytes 1572868

commit v2 on v1

--- a/solution.py
+++ b/solution.py
@@ -13,8 +13,7 @@
 TAPS = 128
 ITERS = 2
 CHUNKS = 4
-UNROLL = 4
-HIGH = lax.Precision.HIGHEST
+UNROLL = 8
 MESH = pl.DeviceIdType.MESH
 F32, BF16 = jnp.float32, jnp.bfloat16
 LANES = (((1,), (1,)), ((), ()))
@@ -33,11 +32,30 @@
     return table.transpose(0, 2, 1, 3).reshape(NF, TAPS, 2 * TAPS).astype(BF16)
 
 
+def split(value):
+    high = value.astype(BF16)
+    return high, (value - high.astype(F32)).astype(BF16)
+
+
+def gram_of(value):
+    n = value.shape[0]
+    both = jnp.concatenate(split(value), axis=0)
+    out = lax.dot_general(both, both, LANES, preferred_element_type=F32)
+    return (out[:n, :n] + out[n:, n:]) + (out[:n, n:] + out[n:, :n])
+
+
+def product(left, right):
+    (a, b), (c, d) = split(left), split(right)
+    return jnp.dot(
+        jnp.concatenate([a, b, a], axis=1), jnp.concatenate([c, c, d], axis=0), preferred_element_type=F32
+    )
+
+
 def kernel(
     sizes,
     sig_ref, w_ref, h_ref, circ_ref,
     w_out, h_out,
-    circ, table, halo, lhs, spec, ratios, sums, grams, acc, subs, parts, wt,
+    circ, table, halo, lhs, spec, ratios, sums, grams, acc, subs, parts, wt, outer, inner,
     circ_sem, halo_send, halo_recv, sum_send, sum_recv, gram_send, gram_recv,
     sub_send, sub_recv, part_send, part_recv, w_send, w_recv,
 ):
@@ -66,7 +84,10 @@
 
     grams[...] = jnp.zeros_like(grams)
     acc[...] = jnp.zeros_like(acc)
-    wt[0] = w_ref[...]
+    outer[...] = w_ref[...].T
+    for f in range(NF):
+        inner[f * channels : (f + 1) * channels, :] = outer[pl.ds(f, channels, stride=NF), :]
+    wt[0] = inner[...].T
 
     barrier = pltpu.get_barrier_semaphore()
     for name, size in (("frm", nfrm), ("row", nrow), ("sub", nsub)):
@@ -101,7 +122,7 @@
 
     def share_gram(it):
         now = wt[it]
-        grams[it, row, :, 0:rank] = lax.dot_general(now, now, LANES, precision=HIGH, preferred_element_type=F32)
+        grams[it, row, :, 0:rank] = gram_of(now)
         return [
             push(grams.at[it, row], grams.at[it, row], gram_send.at[it, s - 1], gram_recv.at[it, s - 1], {"row": peer("row", s)})
             for s in range(1, nrow)
@@ -207,7 +228,7 @@
     def ratio(it, q, gram):
         cols = slice(q * wide, (q + 1) * wide)
         old = h_ref[:, cols] if it == 0 else h_out[:, cols]
-        ratios[:, cols] = old / jnp.dot(gram, old, precision=HIGH, preferred_element_type=F32)
+        ratios[:, cols] = old / product(gram, old)
 
     def update_h(it, q, copies):
         for copy in copies:
@@ -218,7 +239,7 @@
         cols = slice(q * wide, (q + 1) * wide)
         new = ratios[:, cols] * total
         acc[it, :, 0:rows] += lax.dot_general(new.astype(BF16), spec[:, cols], LANES, preferred_element_type=F32)
-        acc[it, :, rows : rows + rank] += lax.dot_general(new, new, LANES, precision=HIGH, preferred_element_type=F32)
+        acc[it, :, rows : rows + rank] += gram_of(new)
 
     def finish_h(it, q, copies):
         for copy in copies:
@@ -265,7 +286,7 @@
         for s in range(1, nfrm):
             total = total + parts[it, s].astype(F32)
         gram = (total[:, rows:] + pltpu.roll(total[:, rows:], 128 - rank, 1))[:, :rank]
-        den = jnp.dot(gram, wt[it], precision=HIGH, preferred_element_type=F32)
+        den = product(gram, wt[it])
         wt[it + 1, mine, :] = wt[it, mine, :] * total[:, :rows] / den
         copies = [
             push(wt.at[it + 1, mine], wt.at[it + 1, mine], w_send.at[it, s - 1], w_recv.at[it, s - 1], {"sub": peer("sub", s)})
@@ -318,7 +339,10 @@
                 finish_h(it, q, trailing[q])
 
         update_w(it, meanwhile)
-    w_out[...] = wt[ITERS]
+    inner[...] = wt[ITERS].T
+    for c in range(channels):
+        outer[c * NF : (c + 1) * NF, :] = inner[pl.ds(c, NF, stride=channels), :]
+    w_out[...] = outer[...].T
 
     for copy in sent:
         copy.wait_send()
@@ -341,7 +365,6 @@
         rows, rank = w_start.shape
         half = rank // nsub
         wide = frames // CHUNKS
-        w = w_start.reshape(channels, NF, rank).transpose(2, 1, 0).reshape(rank, rows)
         dma = pltpu.SemaphoreType.DMA
         vmem = pl.BlockSpec(memory_space=pltpu.VMEM)
         w, h = pl.pallas_call(
@@ -365,6 +388,8 @@
                 pltpu.VMEM((ITERS, nsub - 1, half, rows + 128), F32),
                 pltpu.VMEM((ITERS, nfrm, half, rows + 128), BF16),
                 pltpu.VMEM((ITERS + 1, rank, rows), F32),
+                pltpu.VMEM((rows, rank), F32),
+                pltpu.VMEM((rows, rank), F32),
                 dma,
                 dma((2,)), dma((2,)),
                 dma((ITERS, 2, CHUNKS, nrow - 1)), dma((ITERS, 2, CHUNKS, nrow - 1)),
@@ -376,8 +401,8 @@
             compiler_params=pltpu.CompilerParams(
                 collective_id=0, has_side_effects=True, vmem_limit_bytes=56 << 20
             ),
-        )(signal, w, h_start, jnp.asarray(circ))
-        return w.reshape(rank, NF, channels).transpose(2, 1, 0).reshape(rows, rank), h
+        )(signal, w_start.T, h_start, jnp.asarray(circ))
+        return w.T, h
 
     return jax.shard_map(
         shards,

time: 61.8 us -> 57.2 us (0.926)
  Pallas kernels: 55.4 us -> 52.9 us
  local copies, waits for them, and re-layouts: 5.59 us -> 3.46 us
    reshape x5 -> x0, local copies, waits for them, and re-layouts: 4.58 us -> none  [the longest x3 2.43 us: shards(): w_start.reshape(channels, NF, rank).transpose(2, 1, 0).reshape(rank, rows)]
    unnamed x3 -> x2, local copies, waits for them, and re-layouts: 0.8 us -> 3.46 us
    pallas_call x1, Pallas kernels: 55.4 us -> 52.9 us  [shards(): pl.pallas_call(functools.partial(kernel, sizes), out_shape=(jax.ShapeDtyp...]
where the time goes in v2:
time: 57.2 us; the launch traced here: 57 us
  Pallas kernels  52.9 us (92%)
  local copies, waits for them, and re-layouts  3.46 us (6%)
  between operations  0.64 us (1%)
    pallas_call x1, Pallas kernels, shards(): pl.pallas_call(functools.partial(kernel, sizes), out_shape=(jax.ShapeDtyp...  52.9 us
    unnamed x2, local copies, waits for them, and re-layouts  3.46 us

profile of v2, /device:TPU:0, one launch (start us, length us, event | category | flops | bytes accessed | tf_op | source)
XLA Modules:
  0.0 57.0 jit_solution(6326309296958633597)
XLA Ops:
  0.6 52.9 %shard_map.59 = (f32[32,1280]{1,0:T(8,128)}, f32[32,4096]{1,0:T(8,128)}) custom-call(bf16[32,4096]{1,0:T(8,128)(2,1)} %sig_ref.1, f32[32,1280]{1,0:T(8,128)} %bitcast.2, f32[32,4096]{1,0:T(8,128)} %h_ref.1, bf16[40,128,256]{2,1,0:T(8,128)(2,1)} %constant.2.clone.circ_ref), custom_call_target="tpu_custom_call" | custom-call | tf_op jit(solution)/shard_map/pallas_call | solution.py:370
  53.5 1.6 %copy.8 = f32[1280,32]{0,1:T(8,128)} copy(f32[1280,32]{0,1:T(8,128)} %bitcast.3) | data formatting | bytes 327680
  55.1 1.9 %copy.9 = f32[32,4096]{1,0:T(8,128)} copy(f32[32,4096]{1,0:T(8,128)} %get-tuple-element.9) | data formatting | bytes 1048576

commit v3 on v2

--- a/solution.py
+++ b/solution.py
@@ -354,6 +354,11 @@
     @pl.when(has_left)
     def _():
         edge(-1).wait_send()
+
+
+def settle(w_ref, h_ref, w_out, h_out):
+    w_out[...] = w_ref[...]
+    h_out[...] = h_ref[...]
 
 
 def solution(mesh):
@@ -402,6 +407,12 @@
                 collective_id=0, has_side_effects=True, vmem_limit_bytes=56 << 20
             ),
         )(signal, w_start.T, h_start, jnp.asarray(circ))
+        w, h = pl.pallas_call(
+            settle,
+            out_shape=(jax.ShapeDtypeStruct(w.shape, F32), jax.ShapeDtypeStruct(h.shape, F32)),
+            in_specs=[vmem, vmem],
+            out_specs=(vmem, vmem),
+        )(w, h)
         return w.T, h
 
     return jax.shard_map(

time: 57.2 us -> 55.7 us (0.974)
  local copies, waits for them, and re-layouts: 3.46 us -> 0 us
  Pallas kernels: 52.9 us -> 54.8 us
    unnamed x2 -> x0, local copies, waits for them, and re-layouts: 3.46 us -> none
    pallas_call x0 -> x1, Pallas kernels: none -> 1.99 us  [shards(): pl.pallas_call(settle, out_shape=(jax.ShapeDtypeStruct(w.shape, F32), jax...]
where the time goes in v3:
time: 55.7 us; the launch traced here: 55.5 us
  Pallas kernels  54.8 us (98%)
  between operations  0.64 us (1%)
    pallas_call x1, Pallas kernels, shards(): pl.pallas_call(functools.partial(kernel, sizes), out_shape=(jax.ShapeDtyp...  52.9 us
    pallas_call x1, Pallas kernels, shards(): pl.pallas_call(settle, out_shape=(jax.ShapeDtypeStruct(w.shape, F32), jax...  1.99 us

profile of v3, /device:TPU:0, one launch (start us, length us, event | category | flops | bytes accessed | tf_op | source)
XLA Modules:
  0.0 55.5 jit_solution(14105491245322950699)
XLA Ops:
  0.6 52.9 %shard_map.59 = (f32[32,1280]{1,0:T(8,128)}, f32[32,4096]{1,0:T(8,128)}) custom-call(bf16[32,4096]{1,0:T(8,128)(2,1)} %sig_ref.1, f32[32,1280]{1,0:T(8,128)} %bitcast.2, f32[32,4096]{1,0:T(8,128)} %h_ref.1, bf16[40,128,256]{2,1,0:T(8,128)(2,1)} %constant.2.clone.circ_ref), custom_call_target="tpu_custom_call" | custom-call | tf_op jit(solution)/shard_map/pallas_call | solution.py:375
  53.5 2.0 %shard_map.60 = (f32[32,1280]{1,0:T(8,128)}, f32[32,4096]{1,0:T(8,128)}) custom-call(f32[32,1280]{1,0:T(8,128)} %get-tuple-element.6.w_ref, f32[32,4096]{1,0:T(8,128)} %get-tuple-element.7.h_ref), custom_call_target="tpu_custom_call" | custom-call | tf_op jit(solution)/shard_map/pallas_call | solution.py:410
